TPU v7x, 256 devices: a whole 4x4x8 slice. The times are simulated.
256 devices in a mesh: seq: 32 (over z, y_hi, core), ch: 8 (over y_lo, x).
Axes of the slice: x: 4, y: 4 (y_hi: 2, y_lo: 2; y = y_hi * 2 + y_lo), z: 8, core: 2. Of those that a mesh axis runs over, the one named last changes fastest.
Arguments:
- tokens: int32 [16384], P('seq'), may hold values from 0 to 4
- embedding: bfloat16 [5, 1024], P(None, 'ch'), may hold values from -4 to 4
- taps_dilated: float32 [3, 1024], P(None, 'ch'), may hold values from -3.5 to 3.5
- taps_short: float32 [3, 1024], P(None, 'ch'), may hold values from -3.5 to 3.5
- long_filter: float32 [16384, 1024], P('seq', 'ch'), may hold values from -1.5 to 1.5
- cotangent: bfloat16 [16384, 1024], P('seq', 'ch'), may hold values from -0.046875 to 0.046875
Outputs:
- mixed: bfloat16 [16384, 1024], P('seq', 'ch')
- filter_grad: float32 [16384, 1024], P('seq', 'ch')
All inputs are finite; a program needn't handle non-finite values.
Results may differ from a plain program's by a relative error of at most 0.001.
Values may be sent and summed in bfloat16 or wider, within the bound.
A program may use at most 128 MiB of HBM per device.

v0:
```python
import functools
import math

import jax
import jax.numpy as jnp
import numpy as np
from jax import lax
from jax.experimental import pallas as pl
from jax.experimental.pallas import tpu as pltpu
from jax.sharding import PartitionSpec as P

SHORT_DILATION = 8
LANES = 128
TILE = 8
MESH = pl.DeviceIdType.MESH


def split_table(table):
    high = table.astype(np.float32).astype(jnp.bfloat16)
    low = (table - high.astype(np.float64)).astype(np.float32).astype(jnp.bfloat16)
    return np.stack([high, low])


@functools.lru_cache(maxsize=None)
def dft_tables(seq_count, rows_per_block):
    rows = seq_count * rows_per_block
    total = rows * LANES
    k1 = np.arange(rows)
    angle = 2.0 * math.pi * ((np.arange(rows)[None, :] * (4 * k1[:, None] + 1)) % (4 * rows)) / (4 * rows)
    first = np.zeros((2, 2, rows, seq_count, 2, rows_per_block))
    for jj in range(2):
        first[jj, 0, :, :, jj, :] = np.cos(angle).reshape(rows, seq_count, rows_per_block)
        first[jj, 1, :, :, jj, :] = -np.sin(angle).reshape(rows, seq_count, rows_per_block)
    first = first.reshape(4 * rows, 2 * rows)
    n2 = np.arange(LANES)
    turn = 2.0 * math.pi * ((n2[None, :] * (4 * k1[:, None] + 1)) % (4 * total)) / (4 * total)
    twiddle = np.stack([np.cos(turn), -np.sin(turn)]).astype(np.float32)
    lane_angle = 2.0 * math.pi * ((n2[:, None] * n2[None, :]) % LANES) / LANES
    cos, sin = np.cos(lane_angle), np.sin(lane_angle)
    second = np.block([[cos, -sin], [sin, cos]])
    return (
        split_table(first),
        twiddle,
        split_table(second),
        split_table(second.T),
        split_table(first.T / total),
    )


class Place:
    def __init__(self, seq_count, ch_count):
        self.seq_count, self.ch_count = seq_count, ch_count
        self.members = 2 * seq_count
        self.s, self.c = lax.axis_index("seq"), lax.axis_index("ch")
        self.low = jnp.minimum(self.c, ch_count - 1 - self.c)
        self.side = jnp.where(2 * self.c >= ch_count, 1, 0)
        self.g = self.side * seq_count + self.s

    def peer(self, step):
        member = lax.rem(self.g + step, self.members)
        side = lax.div(member, self.seq_count)
        return member, side, lax.rem(member, self.seq_count)

    def device(self, side, s):
        return (s, self.low + side * (self.ch_count - 1 - 2 * self.low))

    def chunk_of(self, member, side):
        return member + side * (self.members - 1 - 2 * member)


def greet(place):
    barrier = pltpu.get_barrier_semaphore()

    def signal(step, carry):
        _, side, s = place.peer(step)
        pl.semaphore_signal(barrier, inc=1, device_id=place.device(side, s), device_id_type=MESH)
        return carry

    lax.fori_loop(1, place.members, signal, 0)
    return lambda: pl.semaphore_wait(barrier, place.members - 1)


def await_bytes(ref, sem):
    pltpu.make_async_copy(ref, ref, sem).wait()


def spread_kernel(seq_count, ch_count, tok_ref, par_ref, cot_ref, filt_ref, tok_all, par_all, cot_all, filt_all,
                  cot_send, filt_send, turned, send_sem, recv_sem):
    place = Place(seq_count, ch_count)
    await_all = greet(place)
    width = cot_ref.shape[1]
    parts = cot_ref.shape[0] // LANES
    chunks = cot_send.shape
    for r in range(parts):
        turned[pl.ds(r, width, stride=parts), :] = cot_ref[pl.ds(r * LANES, LANES), :].astype(jnp.float32).T
    cot_send[...] = turned[...].reshape(chunks).astype(jnp.bfloat16)
    for r in range(parts):
        filt_send[pl.ds(r, width, stride=parts), :] = filt_ref[pl.ds(r * LANES, LANES), :].T
    await_all()

    mirror = place.device(1 - place.side, place.s)
    params = pltpu.make_async_remote_copy(
        src_ref=par_ref, dst_ref=par_all.at[place.side], send_sem=send_sem.at[0], recv_sem=recv_sem.at[0],
        device_id=mirror, device_id_type=MESH)
    params.start()
    own_params = pltpu.make_async_copy(par_ref, par_all.at[place.side], send_sem.at[4])
    own_params.start()

    def send_tokens(step, carry):
        s = lax.rem(place.s + step, seq_count)
        pltpu.make_async_remote_copy(
            src_ref=tok_ref, dst_ref=tok_all.at[place.s], send_sem=send_sem.at[1], recv_sem=recv_sem.at[1],
            device_id=place.device(place.side, s), device_id_type=MESH).start()
        return carry

    lax.fori_loop(1, seq_count, send_tokens, 0)
    pltpu.make_async_copy(tok_ref, tok_all.at[place.s], recv_sem.at[1]).start()

    def rows_of(chunk):
        return pl.ds(pl.multiple_of(chunk * TILE, TILE), TILE)

    def send(step, carry):
        member, side, s = place.peer(step)
        chunk = place.chunk_of(member, place.side)
        device = place.device(side, s)
        pltpu.make_async_remote_copy(
            src_ref=filt_send.at[rows_of(chunk)], dst_ref=filt_all.at[rows_of(place.g)], send_sem=send_sem.at[3],
            recv_sem=recv_sem.at[3], device_id=device, device_id_type=MESH).start()
        pltpu.make_async_remote_copy(
            src_ref=cot_send.at[chunk], dst_ref=cot_all.at[place.g], send_sem=send_sem.at[2],
            recv_sem=recv_sem.at[2], device_id=device, device_id_type=MESH).start()
        return carry

    def send_pair(step, carry):
        send(step, carry)
        return send(place.members - step, carry)

    lax.fori_loop(1, seq_count, send_pair, 0)
    send(seq_count, 0)
    own = place.chunk_of(place.g, place.side)
    pltpu.make_async_copy(cot_send.at[own], cot_all.at[place.g], recv_sem.at[2]).start()
    pltpu.make_async_copy(filt_send.at[rows_of(own)], filt_all.at[rows_of(place.g)], recv_sem.at[3]).start()

    own_params.wait()
    params.wait()
    await_bytes(tok_all, recv_sem.at[1])
    await_bytes(cot_all, recv_sem.at[2])
    await_bytes(filt_all, recv_sem.at[3])
    await_bytes(tok_all.at[pl.ds(0, seq_count - 1)], send_sem.at[1])
    await_bytes(cot_send.at[pl.ds(0, place.members - 1)], send_sem.at[2])
    await_bytes(filt_send.at[pl.ds(0, TILE * (place.members - 1))], send_sem.at[3])


def split(x):
    high = x.astype(jnp.bfloat16)
    return high, (x - high.astype(jnp.float32)).astype(jnp.bfloat16)


def dot(a, b):
    return jnp.dot(a, b, preferred_element_type=jnp.float32)


def dot_left(table, x):
    high, low = split(x)
    return dot(table[0], high) + (dot(table[0], low) + dot(table[1], high))


def dot_right(x, table):
    high, low = split(x)
    return dot(high, table[0]) + (dot(high, table[1]) + dot(low, table[0]))


def shifted(x, amount, lane, row, parts):
    count = x.shape[0]
    zero = jnp.zeros_like(x[:1])
    if amount > 0:
        rolled = pltpu.roll(x, amount, axis=2)
        before = jnp.concatenate([zero, rolled[: count - 1]], axis=0)
        lower = jnp.where(row % parts == 0, pltpu.roll(before, parts + 1, axis=1), pltpu.roll(rolled, 1, axis=1))
        return jnp.where(lane >= amount, rolled, lower)
    rolled = pltpu.roll(x, LANES + amount, axis=2)
    after = jnp.concatenate([rolled[1:], zero], axis=0)
    upper = jnp.where(row % parts == parts - 1, pltpu.roll(after, parts - 1, axis=1), pltpu.roll(rolled, TILE - 1, axis=1))
    return jnp.where(lane < LANES + amount, rolled, upper)


def turn_kernel(seq_count, ch_count, kernel_count, nuc_count, tok_ref, par_ref, cot_ref, filt_ref, first_ref, twiddle_ref,
                second_ref, second_back_ref, first_back_ref, mixed_ref, grad_ref, hidden_ref, spec_ref):
    place = Place(seq_count, ch_count)
    rows = spec_ref.shape[1]
    parts = rows // seq_count
    flat = (seq_count * TILE, LANES)
    tiles = (seq_count, TILE, LANES)
    lane = lax.broadcasted_iota(jnp.int32, (1, TILE, LANES), 2)
    row = lax.broadcasted_iota(jnp.int32, (1, TILE, LANES), 1)
    width = par_ref.shape[2]
    par_lane = lax.broadcasted_iota(jnp.int32, (TILE, width), 1)
    par_row = lax.broadcasted_iota(jnp.int32, (TILE, width), 0)
    tokens = tok_ref[...]
    turn_re, turn_im = twiddle_ref[0], twiddle_ref[1]

    values = []
    for side in range(2):
        chunk = place.g if side == 0 else place.members - 1 - place.g
        here = par_lane == 2 * chunk + par_row // parts
        values.append([
            jnp.sum(jnp.where(here, par_ref[side, pl.ds(k, 1), :], 0.0), axis=1, keepdims=True)[None]
            for k in range(nuc_count + 2 * kernel_count)
        ])
    for side in range(2):
        hidden = jnp.zeros(tiles, jnp.float32)
        for letter in range(nuc_count):
            hidden = jnp.where(tokens == letter, values[side][letter], hidden)
        hidden_ref[side] = hidden

    def fir(side, tap_side, sign):
        taps = values[tap_side][nuc_count:]
        if tap_side != side:
            taps = [jnp.where(row < parts, t[:, TILE - 1:, :], t[:, :1, :]) for t in taps]
        source = hidden_ref[side]
        inner = taps[0] * source
        for k in range(1, kernel_count):
            inner = inner + taps[k] * shifted(source, sign * k * SHORT_DILATION, lane, row, parts)
        taps = taps[kernel_count:]
        conv = taps[0] * inner
        for k in range(1, kernel_count):
            conv = conv + taps[k] * shifted(inner, sign * k, lane, row, parts)
        return conv.reshape(flat)

    def transform(pair, slots):
        both = jnp.concatenate(pair, axis=1)
        section = dot_left(first_ref, both)
        stack = []
        for index in range(2):
            cols = slice(index * LANES, (index + 1) * LANES)
            for jj in range(2):
                re = section[2 * jj * rows:(2 * jj + 1) * rows, cols]
                im = section[(2 * jj + 1) * rows:(2 * jj + 2) * rows, cols]
                stack.append(jnp.concatenate([re * turn_re - im * turn_im, re * turn_im + im * turn_re], axis=1))
        spec = dot_right(jnp.concatenate(stack, axis=0), second_ref)
        for index in range(2):
            for jj in range(2):
                at = (index * 2 + jj) * rows
                spec_ref[slots[index] + jj] = spec[at:at + rows]

    for side in range(2):
        transform([fir(side, side, 1), fir(side, 1 - side, -1)], (8 * side, 8 * side + 2))
    for side in range(2):
        block = slice(side * seq_count, (side + 1) * seq_count)
        seed = cot_ref[block].astype(jnp.float32) * hidden_ref[side]
        filt = filt_ref[side * seq_count * TILE:(side + 1) * seq_count * TILE]
        transform([filt, seed.reshape(flat)], (8 * side + 4, 8 * side + 6))

    def parts_of(side, kind, jj):
        full = spec_ref[8 * side + 2 * kind + jj]
        return full[:, :LANES], full[:, LANES:]

    def times(a, b):
        return a[0] * b[0] - a[1] * b[1], a[0] * b[1] + a[1] * b[0]

    def times_conj(a, b):
        return a[0] * b[0] + a[1] * b[1], a[1] * b[0] - a[0] * b[1]

    for side in range(2):
        stack = []
        for jj in range(2):
            other = (1 - side, 1 - jj)
            u, v, h, s = [parts_of(side, kind, jj) for kind in range(4)]
            v_far, h_far, s_far = [parts_of(other[0], kind, other[1]) for kind in range(1, 4)]
            long_spec = [x + y for x, y in zip(times(h, u), times_conj(v, h_far))]
            grad_spec = [x + y for x, y in zip(times_conj(s, u), times_conj(v_far, s_far))]
            stack.append(jnp.concatenate(long_spec, axis=1))
            stack.append(jnp.concatenate(grad_spec, axis=1))
        section = dot_right(jnp.concatenate(stack, axis=0), second_back_ref)
        columns = []
        for index in range(2):
            pieces = []
            for jj in range(2):
                at = (2 * jj + index) * rows
                re, im = section[at:at + rows, :LANES], section[at:at + rows, LANES:]
                pieces.append(re * turn_re + im * turn_im)
                pieces.append(im * turn_re - re * turn_im)
            columns.append(jnp.concatenate(pieces, axis=0))
        wave = dot_left(first_back_ref, jnp.concatenate(columns, axis=1))
        block = slice(side * seq_count, (side + 1) * seq_count)
        mixed_ref[block] = (hidden_ref[side] * wave[:, :LANES].reshape(tiles)).astype(jnp.bfloat16)
        grad_ref[side * seq_count * TILE:(side + 1) * seq_count * TILE] = wave[:, LANES:]


def return_kernel(seq_count, ch_count, mixed_ref, grad_ref, mixed_all, grad_all, send_sem, recv_sem):
    place = Place(seq_count, ch_count)
    greet(place)()

    def rows_of(chunk):
        return pl.ds(pl.multiple_of(chunk * TILE, TILE), TILE)

    def send(step, carry):
        member, side, s = place.peer(step)
        chunk = place.chunk_of(place.g, side)
        device = place.device(side, s)
        pltpu.make_async_remote_copy(
            src_ref=grad_ref.at[rows_of(member)], dst_ref=grad_all.at[rows_of(chunk)], send_sem=send_sem.at[1],
            recv_sem=recv_sem.at[1], device_id=device, device_id_type=MESH).start()
        pltpu.make_async_remote_copy(
            src_ref=mixed_ref.at[member], dst_ref=mixed_all.at[chunk], send_sem=send_sem.at[0],
            recv_sem=recv_sem.at[0], device_id=device, device_id_type=MESH).start()
        return carry

    def send_pair(step, carry):
        send(step, carry)
        return send(place.members - step, carry)

    lax.fori_loop(1, seq_count, send_pair, 0)
    send(seq_count, 0)
    own = place.chunk_of(place.g, place.side)
    pltpu.make_async_copy(mixed_ref.at[place.g], mixed_all.at[own], recv_sem.at[0]).start()
    pltpu.make_async_copy(grad_ref.at[rows_of(place.g)], grad_all.at[rows_of(own)], recv_sem.at[1]).start()
    await_bytes(mixed_all, recv_sem.at[0])
    await_bytes(grad_all, recv_sem.at[1])
    await_bytes(mixed_ref.at[pl.ds(0, place.members - 1)], send_sem.at[0])
    await_bytes(grad_ref.at[pl.ds(0, TILE * (place.members - 1))], send_sem.at[1])


def settle_kernel(mixed_all, grad_all, mixed_ref, grad_ref, turned):
    parts = grad_ref.shape[0] // LANES
    width = grad_ref.shape[1]
    turned[...] = mixed_all[...].astype(jnp.float32).reshape(turned.shape)
    for r in range(parts):
        rows = pl.ds(r * LANES, LANES)
        mixed_ref[rows, :] = turned[pl.ds(r, width, stride=parts), :].T.astype(jnp.bfloat16)
        grad_ref[rows, :] = grad_all[pl.ds(r, width, stride=parts), :].T


def local(seq_count, ch_count, tokens, embedding, taps_dilated, taps_short, long_filter, cotangent):
    block_rows, width = cotangent.shape
    kernel_count = taps_dilated.shape[0]
    nuc_count = embedding.shape[0]
    parts = block_rows // LANES
    members = 2 * seq_count
    rows = parts * seq_count
    assert 2 * parts == TILE and width == 2 * members
    vmem = pl.BlockSpec(memory_space=pltpu.VMEM)
    f32, bf16 = jnp.float32, jnp.bfloat16
    shape = jax.ShapeDtypeStruct
    limit = 48 * 1024 * 1024

    own_tokens = tokens.reshape(parts, LANES)
    own_tokens = jnp.concatenate([own_tokens, own_tokens], axis=0)
    used = nuc_count + 2 * kernel_count
    params = jnp.concatenate(
        [embedding.astype(f32), taps_dilated, taps_short, jnp.zeros((-used % TILE, width), f32)], axis=0)

    tok_all, par_all, cot_all, filt_all = pl.pallas_call(
        functools.partial(spread_kernel, seq_count, ch_count),
        out_shape=(
            shape((seq_count, TILE, LANES), jnp.int32),
            shape((2,) + params.shape, f32),
            shape((members, TILE, LANES), bf16),
            shape((members * TILE, LANES), f32),
        ),
        in_specs=[vmem] * 4,
        out_specs=(vmem,) * 4,
        scratch_shapes=[
            pltpu.VMEM((members, TILE, LANES), bf16),
            pltpu.VMEM((members * TILE, LANES), f32),
            pltpu.VMEM((members * TILE, LANES), f32),
            pltpu.SemaphoreType.DMA((5,)),
            pltpu.SemaphoreType.DMA((4,)),
        ],
        compiler_params=pltpu.CompilerParams(collective_id=0, has_side_effects=True, vmem_limit_bytes=limit),
        name="spread",
    )(own_tokens, params, cotangent, long_filter)

    tables = [jnp.asarray(t) for t in dft_tables(seq_count, parts)]
    mixed, grad = pl.pallas_call(
        functools.partial(turn_kernel, seq_count, ch_count, kernel_count, nuc_count),
        out_shape=(shape((members, TILE, LANES), bf16), shape((members * TILE, LANES), f32)),
        in_specs=[vmem] * 9,
        out_specs=(vmem,) * 2,
        scratch_shapes=[
            pltpu.VMEM((2, seq_count, TILE, LANES), f32),
            pltpu.VMEM((16, rows, 2 * LANES), f32),
        ],
        compiler_params=pltpu.CompilerParams(vmem_limit_bytes=limit),
        name="turn",
    )(tok_all, par_all, cot_all, filt_all, *tables)

    mixed_all, grad_all = pl.pallas_call(
        functools.partial(return_kernel, seq_count, ch_count),
        out_shape=(shape((members, TILE, LANES), bf16), shape((members * TILE, LANES), f32)),
        in_specs=[vmem] * 2,
        out_specs=(vmem,) * 2,
        scratch_shapes=[pltpu.SemaphoreType.DMA((2,)), pltpu.SemaphoreType.DMA((2,))],
        compiler_params=pltpu.CompilerParams(collective_id=1, has_side_effects=True, vmem_limit_bytes=limit),
        name="return",
    )(mixed, grad)

    return pl.pallas_call(
        settle_kernel,
        out_shape=(shape((block_rows, width), bf16), shape((block_rows, width), f32)),
        in_specs=[vmem] * 2,
        out_specs=(vmem,) * 2,
        scratch_shapes=[pltpu.VMEM((members * TILE, LANES), f32)],
        name="settle",
    )(mixed_all, grad_all)


def solution(mesh):
    in_specs = (
        P("seq"),
        P(None, "ch"),
        P(None, "ch"),
        P(None, "ch"),
        P("seq", "ch"),
        P("seq", "ch"),
    )
    out_specs = (P("seq", "ch"), P("seq", "ch"))
    body = functools.partial(local, mesh.shape["seq"], mesh.shape["ch"])
    return jax.shard_map(body, mesh=mesh, in_specs=in_specs, out_specs=out_specs, check_vma=False)
```

profile of v0, /device:TPU:1, one launch (start us, length us, event | category | flops | bytes accessed | tf_op | source)
XLA Modules:
  0.0 62.2 jit_solution(13731209476039737855)
XLA Ops:
  0.6 0.0 copy-start.2
  0.7 0.1 pad.3.clone
  0.7 0.8 %pad_add_fusion.tok_ref = s32[8,128]{1,0:T(8,128)S(1)} fusion(s32[4,128]{1,0:T(4,128)} %bitcast.1), kind=kLoop, calls=%fused_computation.1 | loop fusion | flops 1024 | bytes 6144 | tf_op jit(solution)/shard_map/concatenate | solution.py:348
  1.5 0.7 %convert_element_type.3 = f32[5,128]{1,0:T(8,128)S(1)} convert(bf16[5,128]{1,0:T(8,128)(2,1)} %param.12) | non-fusion elementwise | flops 640 | bytes 3840 | tf_op jit(solution)/shard_map/convert_element_type | solution.py:351
  2.2 0.8 %maximum_maximum_fusion.par_ref = f32[16,128]{1,0:T(8,128)S(1)} fusion(f32[3,128]{1,0:T(4,128)} %param.14, f32[3,128]{1,0:T(4,128)} %param.13, f32[5,128]{1,0:T(8,128)S(1)} %convert_element_type.3, f32[16]{0:T(128)S(1)} %pad.3.clone), kind=kLoop, calls=%fused_computation | loop fusion | flops 6144 | bytes 13888 | tf_op jit(solution)/shard_map/concatenate | solution.py:350
  2.9 0.0 copy-start.5
  2.9 0.9 %copy-done.5 = f32[512,128]{1,0:T(8,128)S(1)} copy-done((f32[512,128]{1,0:T(8,128)S(1)}, f32[512,128]{1,0:T(8,128)}, u32[]{:S(2)}) %copy-start.5) | copy-done | bytes 262168
  3.9 0.0 copy-start.6
  3.9 0.9 %copy-done.6 = bf16[512,128]{1,0:T(8,128)(2,1)S(1)} copy-done((bf16[512,128]{1,0:T(8,128)(2,1)S(1)}, bf16[512,128]{1,0:T(8,128)(2,1)}, u32[]{:S(2)}) %copy-start.6) | copy-done | bytes 131096
  4.8 0.0 copy-start.7
  4.8 27.3 %spread.1 = (s32[32,8,128]{2,1,0:T(8,128)S(1)}, f32[2,16,128]{2,1,0:T(8,128)S(1)}, bf16[64,8,128]{2,1,0:T(8,128)(2,1)S(1)}, f32[512,128]{1,0:T(8,128)S(1)}) custom-call(s32[8,128]{1,0:T(8,128)S(1)} %pad_add_fusion.tok_ref, f32[16,128]{1,0:T(8,128)S(1)} %maximum_maximum_fusion.par_ref, bf16[512,128]{1,0:T(8,128)(2,1)S(1)} %copy-done.6, f32[512,128]{1,0:T(8,128)S(1)} %copy-done.5), custom_call_target="tpu_custom_call" | custom-call | tf_op jit(solution)/shard_map/spread/pallas_call | solution.py:353
  32.1 0.0 copy-done.2
  32.1 0.0 copy-done.7
  32.2 0.0 copy-start
  32.2 1.0 %copy-done = bf16[2,256,512]{2,1,0:T(8,128)(2,1)S(1)} copy-done((bf16[2,256,512]{2,1,0:T(8,128)(2,1)S(1)}, bf16[2,256,512]{2,1,0:T(8,128)(2,1)}, u32[]{:S(2)}) %copy-start) | copy-done | bytes 524312
  33.2 0.0 copy-start.1
  33.2 1.0 %copy-done.1 = bf16[2,512,256]{2,1,0:T(8,128)(2,1)S(1)} copy-done((bf16[2,512,256]{2,1,0:T(8,128)(2,1)S(1)}, bf16[2,512,256]{2,1,0:T(8,128)(2,1)}, u32[]{:S(2)}) %copy-start.1) | copy-done | bytes 524312
  34.2 0.0 copy-start.3
  34.2 0.9 %copy-done.3 = bf16[2,256,256]{2,1,0:T(8,128)(2,1)S(1)} copy-done((bf16[2,256,256]{2,1,0:T(8,128)(2,1)S(1)}, bf16[2,256,256]{2,1,0:T(8,128)(2,1)}, u32[]{:S(2)}) %copy-start.3) | copy-done | bytes 262168
  35.2 4.2 %turn.1 = (bf16[64,8,128]{2,1,0:T(8,128)(2,1)S(1)}, f32[512,128]{1,0:T(8,128)S(1)}) custom-call(s32[32,8,128]{2,1,0:T(8,128)S(1)} %get-tuple-element.10.tok_ref, f32[2,16,128]{2,1,0:T(8,128)S(1)} %get-tuple-element.11.par_ref, bf16[64,8,128]{2,1,0:T(8,128)(2,1)S(1)} %get-tuple-element.12.cot_ref, f32[512,128]{1,0:T(8,128)S(1)} %get-tuple-element.13.filt_ref, ...), custom_call_target="tpu_custom_call" | custom-call | tf_op jit(solution)/shard_map/turn/pallas_call | solution.py:375
  39.4 19.6 %return.1 = (bf16[64,8,128]{2,1,0:T(8,128)(2,1)S(1)}, f32[512,128]{1,0:T(8,128)S(1)}) custom-call(bf16[64,8,128]{2,1,0:T(8,128)(2,1)S(1)} %get-tuple-element.14.mixed_ref, f32[512,128]{1,0:T(8,128)S(1)} %get-tuple-element.15.grad_ref), custom_call_target="tpu_custom_call" | custom-call | tf_op jit(solution)/shard_map/return/pallas_call | solution.py:388
  59.0 0.0 copy-start.4
  59.0 0.7 %copy-done.4 = f32[512,128]{1,0:T(8,128)} copy-done((f32[512,128]{1,0:T(8,128)}, f32[512,128]{1,0:T(8,128)S(1)}, u32[]{:S(2)}) %copy-start.4) | copy-done | bytes 262168
  59.7 0.0 copy-start.8
  59.7 0.6 %copy-done.8 = bf16[64,8,128]{2,1,0:T(8,128)(2,1)} copy-done((bf16[64,8,128]{2,1,0:T(8,128)(2,1)}, bf16[64,8,128]{2,1,0:T(8,128)(2,1)S(1)}, u32[]{:S(2)}) %copy-start.8) | copy-done | bytes 131096
  60.3 1.9 %settle.1 = (bf16[512,128]{1,0:T(8,128)(2,1)}, f32[512,128]{1,0:T(8,128)}) custom-call(bf16[64,8,128]{2,1,0:T(8,128)(2,1)} %copy-done.8, f32[512,128]{1,0:T(8,128)} %copy-done.4), custom_call_target="tpu_custom_call" | custom-call | tf_op jit(solution)/shard_map/settle/pallas_call | solution.py:398
  (1 shorter events, 0.0 us)
Async XLA Ops:
  0.6 31.5 %copy-start.2 = (bf16[2,256,256]{2,1,0:T(8,128)(2,1)S(1)}, bf16[2,256,256]{2,1,0:T(8,128)(2,1)}, u32[]{:S(2)}) copy-start(bf16[2,256,256]{2,1,0:T(8,128)(2,1)} %constant.15.clone.second_back_ref) | copy-start | bytes 786436
  2.9 0.9 %copy-start.5 = (f32[512,128]{1,0:T(8,128)S(1)}, f32[512,128]{1,0:T(8,128)}, u32[]{:S(2)}) copy-start(f32[512,128]{1,0:T(8,128)} %filt_ref.1) | copy-start | bytes 786436
  3.9 0.9 %copy-start.6 = (bf16[512,128]{1,0:T(8,128)(2,1)S(1)}, bf16[512,128]{1,0:T(8,128)(2,1)}, u32[]{:S(2)}) copy-start(bf16[512,128]{1,0:T(8,128)(2,1)} %cot_ref.1) | copy-start | bytes 393220
  4.8 27.3 %copy-start.7 = (f32[2,128,128]{2,1,0:T(8,128)S(1)}, f32[2,128,128]{2,1,0:T(8,128)}, u32[]{:S(2)}) copy-start(f32[2,128,128]{2,1,0:T(8,128)} %constant.13.clone.twiddle_ref) | copy-start | bytes 393220
  32.2 1.0 %copy-start = (bf16[2,256,512]{2,1,0:T(8,128)(2,1)S(1)}, bf16[2,256,512]{2,1,0:T(8,128)(2,1)}, u32[]{:S(2)}) copy-start(bf16[2,256,512]{2,1,0:T(8,128)(2,1)} %constant.16.clone.first_back_ref) | copy-start | bytes 1572868
  33.2 1.0 %copy-start.1 = (bf16[2,512,256]{2,1,0:T(8,128)(2,1)S(1)}, bf16[2,512,256]{2,1,0:T(8,128)(2,1)}, u32[]{:S(2)}) copy-start(bf16[2,512,256]{2,1,0:T(8,128)(2,1)} %constant.12.clone.first_ref) | copy-start | bytes 1572868
  34.2 0.9 %copy-start.3 = (bf16[2,256,256]{2,1,0:T(8,128)(2,1)S(1)}, bf16[2,256,256]{2,1,0:T(8,128)(2,1)}, u32[]{:S(2)}) copy-start(bf16[2,256,256]{2,1,0:T(8,128)(2,1)} %constant.14.clone.second_ref) | copy-start | bytes 786436
  59.0 0.7 %copy-start.4 = (f32[512,128]{1,0:T(8,128)}, f32[512,128]{1,0:T(8,128)S(1)}, u32[]{:S(2)}) copy-start(f32[512,128]{1,0:T(8,128)S(1)} %get-tuple-element.17.grad_all) | copy-start | bytes 786436
  59.7 0.6 %copy-start.8 = (bf16[64,8,128]{2,1,0:T(8,128)(2,1)}, bf16[64,8,128]{2,1,0:T(8,128)(2,1)S(1)}, u32[]{:S(2)}) copy-start(bf16[64,8,128]{2,1,0:T(8,128)(2,1)S(1)} %get-tuple-element.16.mixed_all) | copy-start | bytes 393220
where the time goes:
time: 62.6 us; the launch traced here: 62.2 us
  Pallas kernels  53 us (85%)
  local copies, waits for them, and re-layouts  6.32 us (10%)
  other arithmetic  2.22 us (4%)
  between operations  0.71 us (1%)
    pallas_call x1, Pallas kernels, local(): pl.pallas_call(functools.partial(spread_kernel, seq_count, ch_count), out...  27.3 us
    pallas_call x1, Pallas kernels, local(): pl.pallas_call(functools.partial(return_kernel, seq_count, ch_count), out...  19.6 us
    unnamed x18, local copies, waits for them, and re-layouts  6.24 us
    pallas_call x1, Pallas kernels, local(): pl.pallas_call(functools.partial(turn_kernel, seq_count, ch_count, kernel...  4.2 us
    pallas_call x1, Pallas kernels, local(): pl.pallas_call(settle_kernel, out_shape=(shape((block_rows, width), bf16)...  1.91 us

commit v1 on v0

v1 whole, which is shorter than its diff:
```python
import functools
import math

import jax
import jax.numpy as jnp
import numpy as np
from jax import lax
from jax.experimental import pallas as pl
from jax.experimental.pallas import tpu as pltpu
from jax.sharding import PartitionSpec as P

SHORT_DILATION = 8
LANES = 128
TILE = 8
MESH = pl.DeviceIdType.MESH


def split_table(table):
    high = table.astype(np.float32).astype(jnp.bfloat16)
    low = (table - high.astype(np.float64)).astype(np.float32).astype(jnp.bfloat16)
    return np.stack([high, low])


@functools.lru_cache(maxsize=None)
def dft_tables(seq_count, rows_per_block):
    rows = seq_count * rows_per_block
    total = rows * LANES
    k1 = np.arange(rows)
    angle = 2.0 * math.pi * ((np.arange(rows)[None, :] * (4 * k1[:, None] + 1)) % (4 * rows)) / (4 * rows)
    first = np.zeros((2, 2, rows, seq_count, 2, rows_per_block))
    for jj in range(2):
        first[jj, 0, :, :, jj, :] = np.cos(angle).reshape(rows, seq_count, rows_per_block)
        first[jj, 1, :, :, jj, :] = -np.sin(angle).reshape(rows, seq_count, rows_per_block)
    first = first.reshape(4 * rows, 2 * rows)
    n2 = np.arange(LANES)
    turn = 2.0 * math.pi * ((n2[None, :] * (4 * k1[:, None] + 1)) % (4 * total)) / (4 * total)
    twiddle = np.stack([np.cos(turn), -np.sin(turn)]).astype(np.float32)
    lane_angle = 2.0 * math.pi * ((n2[:, None] * n2[None, :]) % LANES) / LANES
    cos, sin = np.cos(lane_angle), np.sin(lane_angle)
    second = np.block([[cos, -sin], [sin, cos]])
    return (
        split_table(first),
        twiddle,
        split_table(second),
        split_table(second.T),
        split_table(first.T / total),
    )


class Place:
    def __init__(self, seq_count, ch_count):
        self.seq_count, self.ch_count = seq_count, ch_count
        self.members = 2 * seq_count
        self.s, self.c = lax.axis_index("seq"), lax.axis_index("ch")
        self.low = jnp.minimum(self.c, ch_count - 1 - self.c)
        self.side = jnp.where(2 * self.c >= ch_count, 1, 0)
        self.g = self.side * seq_count + self.s

    def peer(self, step):
        member = self.g + step
        member = jnp.where(member >= self.members, member - self.members, member)
        side = jnp.where(member >= self.seq_count, 1, 0)
        return member, side, member - side * self.seq_count

    def near(self, step):
        s = self.s + step
        return jnp.where(s >= self.seq_count, s - self.seq_count, s)

    def device(self, side, s):
        return (s, self.low + side * (self.ch_count - 1 - 2 * self.low))

    def chunk_of(self, member, side):
        return member + side * (self.members - 1 - 2 * member)


def greet(place):
    barrier = pltpu.get_barrier_semaphore()

    def signal(step, carry):
        _, side, s = place.peer(step)
        pl.semaphore_signal(barrier, inc=1, device_id=place.device(side, s), device_id_type=MESH)
        return carry

    lax.fori_loop(1, place.members, signal, 0)
    return lambda: pl.semaphore_wait(barrier, place.members - 1)


def await_bytes(ref, sem):
    pltpu.make_async_copy(ref, ref, sem).wait()


def rows_of(chunk):
    return pl.ds(pl.multiple_of(chunk * TILE, TILE), TILE)


def split(x):
    high = x.astype(jnp.bfloat16)
    return high, (x - high.astype(jnp.float32)).astype(jnp.bfloat16)


def dot(a, b):
    return jnp.dot(a, b, preferred_element_type=jnp.float32)


def dot_left(table, x):
    high, low = split(x)
    return dot(table[0], high) + (dot(table[0], low) + dot(table[1], high))


def dot_right(x, table):
    high, low = split(x)
    return dot(high, table[0]) + (dot(high, table[1]) + dot(low, table[0]))


def shifted(x, amount, lane, row, parts):
    count = x.shape[0]
    zero = jnp.zeros_like(x[:1])
    if amount > 0:
        rolled = pltpu.roll(x, amount, axis=2)
        before = jnp.concatenate([zero, rolled[: count - 1]], axis=0)
        lower = jnp.where(row % parts == 0, pltpu.roll(before, parts + 1, axis=1), pltpu.roll(rolled, 1, axis=1))
        return jnp.where(lane >= amount, rolled, lower)
    rolled = pltpu.roll(x, LANES + amount, axis=2)
    after = jnp.concatenate([rolled[1:], zero], axis=0)
    upper = jnp.where(row % parts == parts - 1, pltpu.roll(after, parts - 1, axis=1), pltpu.roll(rolled, TILE - 1, axis=1))
    return jnp.where(lane < LANES + amount, rolled, upper)


def whole_kernel(seq_count, ch_count, tok_ref, emb_ref, dilated_ref, short_ref, cot_hbm, filt_hbm, first_hbm, twiddle_hbm,
                 second_hbm, second_back_hbm, first_back_hbm, mixed_all, grad_all,
                 cot_in, filt_in, turned, tok_send, par_send, cot_send, filt_send, tok_all, par_all, cot_all, filt_all,
                 first_ref, twiddle_ref, second_ref, second_back_ref, first_back_ref, hidden_ref, spec_ref,
                 mixed_ref, grad_ref, load_sem, table_sem, send_sem, recv_sem):
    place = Place(seq_count, ch_count)
    kernel_count, nuc_count = dilated_ref.shape[0], emb_ref.shape[0]
    width = cot_in.shape[1]
    parts = cot_in.shape[0] // LANES
    rows = parts * seq_count
    members = place.members

    load_filt = pltpu.make_async_copy(filt_hbm, filt_in, load_sem.at[0])
    load_cot = pltpu.make_async_copy(cot_hbm, cot_in, load_sem.at[1])
    load_filt.start()
    load_cot.start()
    await_all = greet(place)
    tables = [
        pltpu.make_async_copy(far, near, table_sem.at[index])
        for index, (far, near) in enumerate([
            (first_hbm, first_ref), (twiddle_hbm, twiddle_ref), (second_hbm, second_ref),
            (second_back_hbm, second_back_ref), (first_back_hbm, first_back_ref)])
    ]
    for table in tables:
        table.start()

    par_send[...] = jnp.zeros_like(par_send)
    par_send[pl.ds(0, nuc_count), :] = emb_ref[...].astype(jnp.float32)
    par_send[pl.ds(nuc_count, kernel_count), :] = dilated_ref[...]
    par_send[pl.ds(nuc_count + kernel_count, kernel_count), :] = short_ref[...]
    tok_send[...] = tok_ref[...].astype(jnp.float32).astype(jnp.bfloat16)
    load_filt.wait()
    for r in range(parts):
        filt_send[pl.ds(r, width, stride=parts), :] = filt_in[pl.ds(r * LANES, LANES), :].T
    load_cot.wait()
    for r in range(parts):
        turned[pl.ds(r, width, stride=parts), :] = cot_in[pl.ds(r * LANES, LANES), :].astype(jnp.float32).T
    cot_send[...] = turned[...].reshape(cot_send.shape).astype(jnp.bfloat16)
    await_all()

    params = pltpu.make_async_remote_copy(
        src_ref=par_send, dst_ref=par_all.at[place.side], send_sem=send_sem.at[0], recv_sem=recv_sem.at[0],
        device_id=place.device(1 - place.side, place.s), device_id_type=MESH)
    params.start()
    own_params = pltpu.make_async_copy(par_send, par_all.at[place.side], load_sem.at[2])
    own_params.start()

    def send_tokens(step, carry):
        pltpu.make_async_remote_copy(
            src_ref=tok_send, dst_ref=tok_all.at[place.s], send_sem=send_sem.at[1], recv_sem=recv_sem.at[1],
            device_id=place.device(place.side, place.near(step)), device_id_type=MESH).start()
        return carry

    lax.fori_loop(1, seq_count, send_tokens, 0)
    pltpu.make_async_copy(tok_send, tok_all.at[place.s], recv_sem.at[1]).start()

    def send(step, carry):
        member, side, s = place.peer(step)
        chunk = place.chunk_of(member, place.side)
        device = place.device(side, s)
        pltpu.make_async_remote_copy(
            src_ref=filt_send.at[rows_of(chunk)], dst_ref=filt_all.at[rows_of(place.g)], send_sem=send_sem.at[3],
            recv_sem=recv_sem.at[3], device_id=device, device_id_type=MESH).start()
        pltpu.make_async_remote_copy(
            src_ref=cot_send.at[chunk], dst_ref=cot_all.at[place.g], send_sem=send_sem.at[2],
            recv_sem=recv_sem.at[2], device_id=device, device_id_type=MESH).start()
        return carry

    def send_pair(step, carry):
        send(step, carry)
        return send(members - step, carry)

    lax.fori_loop(1, seq_count, send_pair, 0)
    send(seq_count, 0)
    own = place.chunk_of(place.g, place.side)
    pltpu.make_async_copy(cot_send.at[own], cot_all.at[place.g], recv_sem.at[2]).start()
    pltpu.make_async_copy(filt_send.at[rows_of(own)], filt_all.at[rows_of(place.g)], recv_sem.at[3]).start()

    for table in tables:
        table.wait()
    own_params.wait()
    params.wait()
    await_bytes(tok_all, recv_sem.at[1])

    flat = (seq_count * TILE, LANES)
    tiles = (seq_count, TILE, LANES)
    lane = lax.broadcasted_iota(jnp.int32, (1, TILE, LANES), 2)
    row = lax.broadcasted_iota(jnp.int32, (1, TILE, LANES), 1)
    width = par_all.shape[2]
    par_lane = lax.broadcasted_iota(jnp.int32, (TILE, width), 1)
    par_row = lax.broadcasted_iota(jnp.int32, (TILE, width), 0)
    tokens = tok_all[...].astype(jnp.float32)
    tokens = jnp.concatenate([tokens, tokens], axis=1)
    turn_re, turn_im = twiddle_ref[0], twiddle_ref[1]

    values = []
    for side in range(2):
        chunk = place.g if side == 0 else members - 1 - place.g
        here = par_lane == 2 * chunk + par_row // parts
        values.append([
            jnp.sum(jnp.where(here, par_all[side, pl.ds(k, 1), :], 0.0), axis=1, keepdims=True)[None]
            for k in range(nuc_count + 2 * kernel_count)
        ])
    for side in range(2):
        hidden = jnp.zeros(tiles, jnp.float32)
        for letter in range(nuc_count):
            hidden = jnp.where(tokens == float(letter), values[side][letter], hidden)
        hidden_ref[side] = hidden

    def fir(side, tap_side, sign):
        taps = values[tap_side][nuc_count:]
        if tap_side != side:
            taps = [jnp.where(row < parts, t[:, TILE - 1:, :], t[:, :1, :]) for t in taps]
        source = hidden_ref[side]
        inner = taps[0] * source
        for k in range(1, kernel_count):
            inner = inner + taps[k] * shifted(source, sign * k * SHORT_DILATION, lane, row, parts)
        taps = taps[kernel_count:]
        conv = taps[0] * inner
        for k in range(1, kernel_count):
            conv = conv + taps[k] * shifted(inner, sign * k, lane, row, parts)
        return conv.reshape(flat)

    def transform(pair, slots):
        both = jnp.concatenate(pair, axis=1)
        section = dot_left(first_ref, both)
        stack = []
        for index in range(2):
            cols = slice(index * LANES, (index + 1) * LANES)
            for jj in range(2):
                re = section[2 * jj * rows:(2 * jj + 1) * rows, cols]
                im = section[(2 * jj + 1) * rows:(2 * jj + 2) * rows, cols]
                stack.append(jnp.concatenate([re * turn_re - im * turn_im, re * turn_im + im * turn_re], axis=1))
        spec = dot_right(jnp.concatenate(stack, axis=0), second_ref)
        for index in range(2):
            for jj in range(2):
                at = (index * 2 + jj) * rows
                spec_ref[slots[index] + jj] = spec[at:at + rows]

    for side in range(2):
        transform([fir(side, side, 1), fir(side, 1 - side, -1)], (8 * side, 8 * side + 2))
    await_bytes(cot_all, recv_sem.at[2])
    await_bytes(filt_all, recv_sem.at[3])
    for side in range(2):
        block = slice(side * seq_count, (side + 1) * seq_count)
        seed = cot_all[block].astype(jnp.float32) * hidden_ref[side]
        filt = filt_all[side * seq_count * TILE:(side + 1) * seq_count * TILE]
        transform([filt, seed.reshape(flat)], (8 * side + 4, 8 * side + 6))

    def parts_of(side, kind, jj):
        full = spec_ref[8 * side + 2 * kind + jj]
        return full[:, :LANES], full[:, LANES:]

    def times(a, b):
        return a[0] * b[0] - a[1] * b[1], a[0] * b[1] + a[1] * b[0]

    def times_conj(a, b):
        return a[0] * b[0] + a[1] * b[1], a[1] * b[0] - a[0] * b[1]

    for side in range(2):
        stack = []
        for jj in range(2):
            other = (1 - side, 1 - jj)
            u, v, h, s = [parts_of(side, kind, jj) for kind in range(4)]
            v_far, h_far, s_far = [parts_of(other[0], kind, other[1]) for kind in range(1, 4)]
            long_spec = [x + y for x, y in zip(times(h, u), times_conj(v, h_far))]
            grad_spec = [x + y for x, y in zip(times_conj(s, u), times_conj(v_far, s_far))]
            stack.append(jnp.concatenate(long_spec, axis=1))
            stack.append(jnp.concatenate(grad_spec, axis=1))
        section = dot_right(jnp.concatenate(stack, axis=0), second_back_ref)
        columns = []
        for index in range(2):
            pieces = []
            for jj in range(2):
                at = (2 * jj + index) * rows
                re, im = section[at:at + rows, :LANES], section[at:at + rows, LANES:]
                pieces.append(re * turn_re + im * turn_im)
                pieces.append(im * turn_re - re * turn_im)
            columns.append(jnp.concatenate(pieces, axis=0))
        wave = dot_left(first_back_ref, jnp.concatenate(columns, axis=1))
        block = slice(side * seq_count, (side + 1) * seq_count)
        mixed_ref[block] = (hidden_ref[side] * wave[:, :LANES].reshape(tiles)).astype(jnp.bfloat16)
        grad_ref[side * seq_count * TILE:(side + 1) * seq_count * TILE] = wave[:, LANES:]

        def give_back(step, carry):
            s = place.near(step)
            device = place.device(side, s)
            member = side * seq_count + s
            chunk = place.chunk_of(place.g, side)
            pltpu.make_async_remote_copy(
                src_ref=grad_ref.at[rows_of(member)], dst_ref=grad_all.at[rows_of(chunk)], send_sem=send_sem.at[5],
                recv_sem=recv_sem.at[5], device_id=device, device_id_type=MESH).start()
            pltpu.make_async_remote_copy(
                src_ref=mixed_ref.at[member], dst_ref=mixed_all.at[chunk], send_sem=send_sem.at[4],
                recv_sem=recv_sem.at[4], device_id=device, device_id_type=MESH).start()
            return carry

        def give_pair(step, carry):
            give_back(step, carry)
            return give_back(seq_count - step, carry)

        lax.fori_loop(1, seq_count // 2, give_pair, 0)
        give_back(seq_count // 2, 0)

        @pl.when(place.side == side)
        def _():
            pltpu.make_async_copy(mixed_ref.at[place.g], mixed_all.at[own], recv_sem.at[4]).start()
            pltpu.make_async_copy(grad_ref.at[rows_of(place.g)], grad_all.at[rows_of(own)], recv_sem.at[5]).start()

        @pl.when(place.side != side)
        def _():
            give_back(0, 0)

    await_bytes(tok_all.at[pl.ds(0, seq_count - 1)], send_sem.at[1])
    await_bytes(cot_send.at[pl.ds(0, members - 1)], send_sem.at[2])
    await_bytes(filt_send.at[pl.ds(0, TILE * (members - 1))], send_sem.at[3])
    await_bytes(mixed_ref.at[pl.ds(0, members - 1)], send_sem.at[4])
    await_bytes(grad_ref.at[pl.ds(0, TILE * (members - 1))], send_sem.at[5])
    await_bytes(mixed_all, recv_sem.at[4])
    await_bytes(grad_all, recv_sem.at[5])


def settle_kernel(mixed_all, grad_all, mixed_ref, grad_ref, turned):
    parts = grad_ref.shape[0] // LANES
    width = grad_ref.shape[1]
    turned[...] = mixed_all[...].astype(jnp.float32).reshape(turned.shape)
    for r in range(parts):
        rows = pl.ds(r * LANES, LANES)
        mixed_ref[rows, :] = turned[pl.ds(r, width, stride=parts), :].T.astype(jnp.bfloat16)
        grad_ref[rows, :] = grad_all[pl.ds(r, width, stride=parts), :].T


def local(seq_count, ch_count, tokens, embedding, taps_dilated, taps_short, long_filter, cotangent):
    block_rows, width = cotangent.shape
    kernel_count = taps_dilated.shape[0]
    nuc_count = embedding.shape[0]
    parts = block_rows // LANES
    members = 2 * seq_count
    rows = parts * seq_count
    assert 2 * parts == TILE and width == 2 * members
    vmem = pl.BlockSpec(memory_space=pltpu.VMEM)
    f32, bf16 = jnp.float32, jnp.bfloat16
    shape = jax.ShapeDtypeStruct
    limit = 48 * 1024 * 1024

    any_space = pl.BlockSpec(memory_space=pl.ANY)
    tables = [jnp.asarray(t) for t in dft_tables(seq_count, parts)]
    mixed_all, grad_all = pl.pallas_call(
        functools.partial(whole_kernel, seq_count, ch_count),
        out_shape=(shape((members, TILE, LANES), bf16), shape((members * TILE, LANES), f32)),
        in_specs=[vmem] * 4 + [any_space] * 7,
        out_specs=(vmem,) * 2,
        scratch_shapes=[
            pltpu.VMEM((block_rows, width), bf16),
            pltpu.VMEM((block_rows, width), f32),
            pltpu.VMEM((members * TILE, LANES), f32),
            pltpu.VMEM((parts, LANES), bf16),
            pltpu.VMEM((-(-(nuc_count + 2 * kernel_count) // TILE) * TILE, width), f32),
            pltpu.VMEM((members, TILE, LANES), bf16),
            pltpu.VMEM((members * TILE, LANES), f32),
            pltpu.VMEM((seq_count, parts, LANES), bf16),
            pltpu.VMEM((2, -(-(nuc_count + 2 * kernel_count) // TILE) * TILE, width), f32),
            pltpu.VMEM((members, TILE, LANES), bf16),
            pltpu.VMEM((members * TILE, LANES), f32),
            *[pltpu.VMEM(t.shape, t.dtype) for t in tables],
            pltpu.VMEM((2, seq_count, TILE, LANES), f32),
            pltpu.VMEM((16, rows, 2 * LANES), f32),
            pltpu.VMEM((members, TILE, LANES), bf16),
            pltpu.VMEM((members * TILE, LANES), f32),
            pltpu.SemaphoreType.DMA((3,)),
            pltpu.SemaphoreType.DMA((5,)),
            pltpu.SemaphoreType.DMA((6,)),
            pltpu.SemaphoreType.DMA((6,)),
        ],
        compiler_params=pltpu.CompilerParams(collective_id=0, has_side_effects=True, vmem_limit_bytes=limit),
        name="whole",
    )(tokens.reshape(parts, LANES), embedding, taps_dilated, taps_short, cotangent, long_filter, *tables)

    return pl.pallas_call(
        settle_kernel,
        out_shape=(shape((block_rows, width), bf16), shape((block_rows, width), f32)),
        in_specs=[vmem] * 2,
        out_specs=(vmem,) * 2,
        scratch_shapes=[pltpu.VMEM((members * TILE, LANES), f32)],
        compiler_params=pltpu.CompilerParams(vmem_limit_bytes=8 * 1024 * 1024),
        name="settle",
    )(mixed_all, grad_all)


def solution(mesh):
    in_specs = (
        P("seq"),
        P(None, "ch"),
        P(None, "ch"),
        P(None, "ch"),
        P("seq", "ch"),
        P("seq", "ch"),
    )
    out_specs = (P("seq", "ch"), P("seq", "ch"))
    body = functools.partial(local, mesh.shape["seq"], mesh.shape["ch"])
    return jax.shard_map(body, mesh=mesh, in_specs=in_specs, out_specs=out_specs, check_vma=False)
```

time: 62.6 us -> 52.1 us (0.83)
  Pallas kernels: 53 us -> 41 us
  local copies, waits for them, and re-layouts: 6.32 us -> 9.46 us
  other arithmetic: 2.22 us -> 0 us
    pallas_call x3 -> x1, Pallas kernels: 51.1 us -> 40.1 us  [local(): pl.pallas_call(functools.partial(whole_kernel, seq_count, ch_count), out_...]
    unnamed x18 -> x22, local copies, waits for them, and re-layouts: 6.24 us -> 9.46 us
    concatenate x2 -> x0, other arithmetic: 1.53 us -> none  [the longest x1 0.77 us: local(): jnp.concatenate([embedding.astype(f32), taps_dilated, taps_short, jnp.zer...]
    pallas_call x1, Pallas kernels: 1.91 us -> 0.89 us  [local(): pl.pallas_call(settle_kernel, out_shape=(shape((block_rows, width), bf16)...]
    convert_element_type x1 -> x0, other arithmetic: 0.68 us -> none  [local(): embedding.astype(f32)]
where the time goes in v1:
time: 52.1 us; the launch traced here: 51.1 us
  Pallas kernels  41 us (79%)
  local copies, waits for them, and re-layouts  9.46 us (18%)
  between operations  0.66 us (1%)
    pallas_call x1, Pallas kernels, local(): pl.pallas_call(functools.partial(whole_kernel, seq_count, ch_count), out_...  40.1 us
    unnamed x22, local copies, waits for them, and re-layouts  9.46 us

profile of v1, /device:TPU:1, one launch (start us, length us, event | category | flops | bytes accessed | tf_op | source)
XLA Modules:
  0.0 51.1 jit_solution(15784203324572910356)
XLA Ops:
  0.6 0.0 copy-start
  0.6 1.0 %copy-done = bf16[2,256,512]{2,1,0:T(8,128)(2,1)S(1)} copy-done((bf16[2,256,512]{2,1,0:T(8,128)(2,1)S(1)}, bf16[2,256,512]{2,1,0:T(8,128)(2,1)}, u32[]{:S(2)}) %copy-start) | copy-done | bytes 524312
  1.7 0.0 copy-start.1
  1.7 1.0 %copy-done.1 = bf16[2,512,256]{2,1,0:T(8,128)(2,1)S(1)} copy-done((bf16[2,512,256]{2,1,0:T(8,128)(2,1)S(1)}, bf16[2,512,256]{2,1,0:T(8,128)(2,1)}, u32[]{:S(2)}) %copy-start.1) | copy-done | bytes 524312
  2.7 0.0 copy-start.2
  2.7 0.9 %copy-done.2 = f32[512,128]{1,0:T(8,128)S(1)} copy-done((f32[512,128]{1,0:T(8,128)S(1)}, f32[512,128]{1,0:T(8,128)}, u32[]{:S(2)}) %copy-start.2) | copy-done | bytes 262168
  3.7 0.0 copy-start.3
  3.7 0.9 %copy-done.3 = bf16[2,256,256]{2,1,0:T(8,128)(2,1)S(1)} copy-done((bf16[2,256,256]{2,1,0:T(8,128)(2,1)S(1)}, bf16[2,256,256]{2,1,0:T(8,128)(2,1)}, u32[]{:S(2)}) %copy-start.3) | copy-done | bytes 262168
  4.6 0.0 copy-start.4
  4.6 0.9 %copy-done.4 = bf16[2,256,256]{2,1,0:T(8,128)(2,1)S(1)} copy-done((bf16[2,256,256]{2,1,0:T(8,128)(2,1)S(1)}, bf16[2,256,256]{2,1,0:T(8,128)(2,1)}, u32[]{:S(2)}) %copy-start.4) | copy-done | bytes 262168
  5.6 0.0 copy-start.5
  5.6 0.9 %copy-done.5 = bf16[512,128]{1,0:T(8,128)(2,1)S(1)} copy-done((bf16[512,128]{1,0:T(8,128)(2,1)S(1)}, bf16[512,128]{1,0:T(8,128)(2,1)}, u32[]{:S(2)}) %copy-start.5) | copy-done | bytes 131096
  6.5 0.0 copy-start.6
  6.5 0.9 %copy-done.6 = f32[2,128,128]{2,1,0:T(8,128)S(1)} copy-done((f32[2,128,128]{2,1,0:T(8,128)S(1)}, f32[2,128,128]{2,1,0:T(8,128)}, u32[]{:S(2)}) %copy-start.6) | copy-done | bytes 131096
  7.4 0.0 copy-start.7
  7.4 0.7 %copy-done.7 = s32[512]{0:T(512)S(1)} copy-done((s32[512]{0:T(512)S(1)}, s32[512]{0:T(512)}, u32[]{:S(2)}) %copy-start.7) | copy-done | bytes 2072
  8.1 0.0 copy-start.8
  8.1 0.7 %copy-done.8 = bf16[5,128]{1,0:T(8,128)(2,1)S(1)} copy-done((bf16[5,128]{1,0:T(8,128)(2,1)S(1)}, bf16[5,128]{1,0:T(8,128)(2,1)}, u32[]{:S(2)}) %copy-start.8) | copy-done | bytes 1304
  8.7 0.0 copy-start.9
  8.7 0.7 %copy-done.9 = f32[3,128]{1,0:T(4,128)S(1)} copy-done((f32[3,128]{1,0:T(4,128)S(1)}, f32[3,128]{1,0:T(4,128)}, u32[]{:S(2)}) %copy-start.9) | copy-done | bytes 1560
  9.4 0.0 copy-start.10
  9.4 0.7 %copy-done.10 = f32[3,128]{1,0:T(4,128)S(1)} copy-done((f32[3,128]{1,0:T(4,128)S(1)}, f32[3,128]{1,0:T(4,128)}, u32[]{:S(2)}) %copy-start.10) | copy-done | bytes 1560
  10.1 40.1 %whole.1 = (bf16[64,8,128]{2,1,0:T(8,128)(2,1)S(1)}, f32[512,128]{1,0:T(8,128)S(1)}) custom-call(s32[4,128]{1,0:T(4,128)S(1)} %bitcast.1, bf16[5,128]{1,0:T(8,128)(2,1)S(1)} %copy-done.8, f32[3,128]{1,0:T(4,128)S(1)} %copy-done.9, f32[3,128]{1,0:T(4,128)S(1)} %copy-done.10, bf16[512,128]{1,0:T(8,128)(2,1)S(1)} %copy-done.5, f32[512,128]{1,0:T(8,128)S(1)} %copy-done.2, ...), custom_call_target="tpu_custom_call" | custom-call | tf_op jit(solution)/shard_map/whole/pallas_call | solution.py:376
  50.3 0.9 %settle.1 = (bf16[512,128]{1,0:T(8,128)(2,1)}, f32[512,128]{1,0:T(8,128)}) custom-call(bf16[64,8,128]{2,1,0:T(8,128)(2,1)S(1)} %get-tuple-element.4.mixed_all, f32[512,128]{1,0:T(8,128)S(1)} %get-tuple-element.5.grad_all), custom_call_target="tpu_custom_call" | custom-call | tf_op jit(solution)/shard_map/settle/pallas_call | solution.py:407
Async XLA Ops:
  0.6 1.0 %copy-start = (bf16[2,256,512]{2,1,0:T(8,128)(2,1)S(1)}, bf16[2,256,512]{2,1,0:T(8,128)(2,1)}, u32[]{:S(2)}) copy-start(bf16[2,256,512]{2,1,0:T(8,128)(2,1)} %constant.14.clone.first_back_hbm) | copy-start | bytes 1572868
  1.7 1.0 %copy-start.1 = (bf16[2,512,256]{2,1,0:T(8,128)(2,1)S(1)}, bf16[2,512,256]{2,1,0:T(8,128)(2,1)}, u32[]{:S(2)}) copy-start(bf16[2,512,256]{2,1,0:T(8,128)(2,1)} %constant.10.clone.first_hbm) | copy-start | bytes 1572868
  2.7 0.9 %copy-start.2 = (f32[512,128]{1,0:T(8,128)S(1)}, f32[512,128]{1,0:T(8,128)}, u32[]{:S(2)}) copy-start(f32[512,128]{1,0:T(8,128)} %filt_hbm.1) | copy-start | bytes 786436
  3.7 0.9 %copy-start.3 = (bf16[2,256,256]{2,1,0:T(8,128)(2,1)S(1)}, bf16[2,256,256]{2,1,0:T(8,128)(2,1)}, u32[]{:S(2)}) copy-start(bf16[2,256,256]{2,1,0:T(8,128)(2,1)} %constant.13.clone.second_back_hbm) | copy-start | bytes 786436
  4.6 0.9 %copy-start.4 = (bf16[2,256,256]{2,1,0:T(8,128)(2,1)S(1)}, bf16[2,256,256]{2,1,0:T(8,128)(2,1)}, u32[]{:S(2)}) copy-start(bf16[2,256,256]{2,1,0:T(8,128)(2,1)} %constant.12.clone.second_hbm) | copy-start | bytes 786436
  5.6 0.9 %copy-start.5 = (bf16[512,128]{1,0:T(8,128)(2,1)S(1)}, bf16[512,128]{1,0:T(8,128)(2,1)}, u32[]{:S(2)}) copy-start(bf16[512,128]{1,0:T(8,128)(2,1)} %cot_hbm.1) | copy-start | bytes 393220
  6.5 0.9 %copy-start.6 = (f32[2,128,128]{2,1,0:T(8,128)S(1)}, f32[2,128,128]{2,1,0:T(8,128)}, u32[]{:S(2)}) copy-start(f32[2,128,128]{2,1,0:T(8,128)} %constant.11.clone.twiddle_hbm) | copy-start | bytes 393220
  7.4 0.7 %copy-start.7 = (s32[512]{0:T(512)S(1)}, s32[512]{0:T(512)}, u32[]{:S(2)}) copy-start(s32[512]{0:T(512)} %param.11) | copy-start | bytes 6148
  8.1 0.7 %copy-start.8 = (bf16[5,128]{1,0:T(8,128)(2,1)S(1)}, bf16[5,128]{1,0:T(8,128)(2,1)}, u32[]{:S(2)}) copy-start(bf16[5,128]{1,0:T(8,128)(2,1)} %emb_ref.1) | copy-start | bytes 3844
  8.7 0.7 %copy-start.9 = (f32[3,128]{1,0:T(4,128)S(1)}, f32[3,128]{1,0:T(4,128)}, u32[]{:S(2)}) copy-start(f32[3,128]{1,0:T(4,128)} %dilated_ref.1) | copy-start | bytes 4612
  9.4 0.7 %copy-start.10 = (f32[3,128]{1,0:T(4,128)S(1)}, f32[3,128]{1,0:T(4,128)}, u32[]{:S(2)}) copy-start(f32[3,128]{1,0:T(4,128)} %short_ref.1) | copy-start | bytes 4612

commit v2 on v1

--- a/solution.py
+++ b/solution.py
@@ -126,11 +126,11 @@
     return jnp.where(lane < LANES + amount, rolled, upper)
 
 
-def whole_kernel(seq_count, ch_count, tok_ref, emb_ref, dilated_ref, short_ref, cot_hbm, filt_hbm, first_hbm, twiddle_hbm,
+def whole_kernel(seq_count, ch_count, tok_hbm, emb_hbm, dilated_hbm, short_hbm, cot_hbm, filt_hbm, first_hbm, twiddle_hbm,
                  second_hbm, second_back_hbm, first_back_hbm, mixed_all, grad_all,
-                 cot_in, filt_in, turned, tok_send, par_send, cot_send, filt_send, tok_all, par_all, cot_all, filt_all,
+                 tok_ref, emb_ref, dilated_ref, short_ref, cot_in, filt_in, turned, tok_send, par_send, cot_send, filt_send, tok_all, par_all, cot_all, filt_all,
                  first_ref, twiddle_ref, second_ref, second_back_ref, first_back_ref, hidden_ref, spec_ref,
-                 mixed_ref, grad_ref, load_sem, table_sem, send_sem, recv_sem):
+                 mixed_ref, grad_ref, small_sem, load_sem, table_sem, send_sem, recv_sem):
     place = Place(seq_count, ch_count)
     kernel_count, nuc_count = dilated_ref.shape[0], emb_ref.shape[0]
     width = cot_in.shape[1]
@@ -142,6 +142,13 @@
     load_cot = pltpu.make_async_copy(cot_hbm, cot_in, load_sem.at[1])
     load_filt.start()
     load_cot.start()
+    small = [
+        pltpu.make_async_copy(far, near, small_sem.at[index])
+        for index, (far, near) in enumerate([
+            (tok_hbm, tok_ref), (emb_hbm, emb_ref), (dilated_hbm, dilated_ref), (short_hbm, short_ref)])
+    ]
+    for load in small:
+        load.start()
     await_all = greet(place)
     tables = [
         pltpu.make_async_copy(far, near, table_sem.at[index])
@@ -152,6 +159,8 @@
     for table in tables:
         table.start()
 
+    for load in small:
+        load.wait()
     par_send[...] = jnp.zeros_like(par_send)
     par_send[pl.ds(0, nuc_count), :] = emb_ref[...].astype(jnp.float32)
     par_send[pl.ds(nuc_count, kernel_count), :] = dilated_ref[...]
@@ -348,14 +357,20 @@
     await_bytes(grad_all, recv_sem.at[5])
 
 
-def settle_kernel(mixed_all, grad_all, mixed_ref, grad_ref, turned):
+def settle_kernel(mixed_hbm, grad_hbm, mixed_ref, grad_ref, mixed_all, grad_all, turned, sem):
     parts = grad_ref.shape[0] // LANES
     width = grad_ref.shape[1]
+    load_mixed = pltpu.make_async_copy(mixed_hbm, mixed_all, sem.at[0])
+    load_grad = pltpu.make_async_copy(grad_hbm, grad_all, sem.at[1])
+    load_mixed.start()
+    load_grad.start()
+    load_mixed.wait()
     turned[...] = mixed_all[...].astype(jnp.float32).reshape(turned.shape)
     for r in range(parts):
-        rows = pl.ds(r * LANES, LANES)
-        mixed_ref[rows, :] = turned[pl.ds(r, width, stride=parts), :].T.astype(jnp.bfloat16)
-        grad_ref[rows, :] = grad_all[pl.ds(r, width, stride=parts), :].T
+        mixed_ref[pl.ds(r * LANES, LANES), :] = turned[pl.ds(r, width, stride=parts), :].T.astype(jnp.bfloat16)
+    load_grad.wait()
+    for r in range(parts):
+        grad_ref[pl.ds(r * LANES, LANES), :] = grad_all[pl.ds(r, width, stride=parts), :].T
 
 
 def local(seq_count, ch_count, tokens, embedding, taps_dilated, taps_short, long_filter, cotangent):
@@ -369,16 +384,20 @@
     vmem = pl.BlockSpec(memory_space=pltpu.VMEM)
     f32, bf16 = jnp.float32, jnp.bfloat16
     shape = jax.ShapeDtypeStruct
-    limit = 48 * 1024 * 1024
-
-    any_space = pl.BlockSpec(memory_space=pl.ANY)
+    limit = 67043328
+
+    far = pl.BlockSpec(memory_space=pltpu.HBM)
     tables = [jnp.asarray(t) for t in dft_tables(seq_count, parts)]
     mixed_all, grad_all = pl.pallas_call(
         functools.partial(whole_kernel, seq_count, ch_count),
         out_shape=(shape((members, TILE, LANES), bf16), shape((members * TILE, LANES), f32)),
-        in_specs=[vmem] * 4 + [any_space] * 7,
-        out_specs=(vmem,) * 2,
+        in_specs=[far] * 11,
+        out_specs=(far,) * 2,
         scratch_shapes=[
+            pltpu.VMEM((parts, LANES), jnp.int32),
+            pltpu.VMEM(embedding.shape, bf16),
+            pltpu.VMEM(taps_dilated.shape, f32),
+            pltpu.VMEM(taps_short.shape, f32),
             pltpu.VMEM((block_rows, width), bf16),
             pltpu.VMEM((block_rows, width), f32),
             pltpu.VMEM((members * TILE, LANES), f32),
@@ -395,6 +414,7 @@
             pltpu.VMEM((16, rows, 2 * LANES), f32),
             pltpu.VMEM((members, TILE, LANES), bf16),
             pltpu.VMEM((members * TILE, LANES), f32),
+            pltpu.SemaphoreType.DMA((4,)),
             pltpu.SemaphoreType.DMA((3,)),
             pltpu.SemaphoreType.DMA((5,)),
             pltpu.SemaphoreType.DMA((6,)),
@@ -407,10 +427,15 @@
     return pl.pallas_call(
         settle_kernel,
         out_shape=(shape((block_rows, width), bf16), shape((block_rows, width), f32)),
-        in_specs=[vmem] * 2,
+        in_specs=[far] * 2,
         out_specs=(vmem,) * 2,
-        scratch_shapes=[pltpu.VMEM((members * TILE, LANES), f32)],
-        compiler_params=pltpu.CompilerParams(vmem_limit_bytes=8 * 1024 * 1024),
+        scratch_shapes=[
+            pltpu.VMEM((members, TILE, LANES), bf16),
+            pltpu.VMEM((members * TILE, LANES), f32),
+            pltpu.VMEM((members * TILE, LANES), f32),
+            pltpu.SemaphoreType.DMA((2,)),
+        ],
+        compiler_params=pltpu.CompilerParams(vmem_limit_bytes=limit),
         name="settle",
     )(mixed_all, grad_all)
 

time: 52.1 us -> 43.5 us (0.83)
  local copies, waits for them, and re-layouts: 9.46 us -> 0 us
  Pallas kernels: 41 us -> 42.1 us
    unnamed x22 -> x0, local copies, waits for them, and re-layouts: 9.46 us -> none
    pallas_call x1, Pallas kernels: 0.89 us -> 1.87 us  [local(): pl.pallas_call(settle_kernel, out_shape=(shape((block_rows, width), bf16)...]
where the time goes in v2:
time: 43.5 us; the launch traced here: 42.7 us
  Pallas kernels  42.1 us (97%)
  between operations  0.64 us (1%)
    pallas_call x1, Pallas kernels, local(): pl.pallas_call(functools.partial(whole_kernel, seq_count, ch_count), out_...  40.2 us
    pallas_call x1, Pallas kernels, local(): pl.pallas_call(settle_kernel, out_shape=(shape((block_rows, width), bf16)...  1.87 us

profile of v2, /device:TPU:1, one launch (start us, length us, event | category | flops | bytes accessed | tf_op | source)
XLA Modules:
  0.0 42.7 jit_solution(9704210056329448740)
XLA Ops:
  0.6 40.2 %whole.1 = (bf16[64,8,128]{2,1,0:T(8,128)(2,1)}, f32[512,128]{1,0:T(8,128)}) custom-call(s32[4,128]{1,0:T(4,128)} %bitcast.1, bf16[5,128]{1,0:T(8,128)(2,1)} %emb_hbm.1, f32[3,128]{1,0:T(4,128)} %dilated_hbm.1, f32[3,128]{1,0:T(4,128)} %short_hbm.1, bf16[512,128]{1,0:T(8,128)(2,1)} %cot_hbm.1, f32[512,128]{1,0:T(8,128)} %filt_hbm.1, ...), custom_call_target="tpu_custom_call" | custom-call | tf_op jit(solution)/shard_map/whole/pallas_call | solution.py:391
  40.8 1.9 %settle.1 = (bf16[512,128]{1,0:T(8,128)(2,1)}, f32[512,128]{1,0:T(8,128)}) custom-call(bf16[64,8,128]{2,1,0:T(8,128)(2,1)} %get-tuple-element.4.mixed_hbm, f32[512,128]{1,0:T(8,128)} %get-tuple-element.5.grad_hbm), custom_call_target="tpu_custom_call" | custom-call | tf_op jit(solution)/shard_map/settle/pallas_call | solution.py:427

commit v3 on v2

--- a/solution.py
+++ b/solution.py
@@ -13,6 +13,8 @@
 LANES = 128
 TILE = 8
 MESH = pl.DeviceIdType.MESH
+COUNTS = 32700.0
+LEAST = 1e-33
 
 
 def split_table(table):
@@ -89,8 +91,16 @@
     pltpu.make_async_copy(ref, ref, sem).wait()
 
 
-def rows_of(chunk):
-    return pl.ds(pl.multiple_of(chunk * TILE, TILE), TILE)
+def steps_for(largest):
+    return COUNTS / largest
+
+
+def fixed_point(x):
+    return jnp.floor(x + 0.5).astype(jnp.int32).astype(jnp.int16)
+
+
+def floating(x):
+    return x.astype(jnp.int32).astype(jnp.float32)
 
 
 def split(x):
@@ -127,10 +137,10 @@
 
 
 def whole_kernel(seq_count, ch_count, tok_hbm, emb_hbm, dilated_hbm, short_hbm, cot_hbm, filt_hbm, first_hbm, twiddle_hbm,
-                 second_hbm, second_back_hbm, first_back_hbm, mixed_all, grad_all,
-                 tok_ref, emb_ref, dilated_ref, short_ref, cot_in, filt_in, turned, tok_send, par_send, cot_send, filt_send, tok_all, par_all, cot_all, filt_all,
+                 second_hbm, second_back_hbm, first_back_hbm, mixed_all, grad_all, grad_size_all,
+                 tok_ref, emb_ref, dilated_ref, short_ref, cot_in, filt_in, turned, tok_send, par_send, cot_send, filt_send, filt_size, tok_all, par_all, cot_all, filt_all, filt_size_all,
                  first_ref, twiddle_ref, second_ref, second_back_ref, first_back_ref, hidden_ref, spec_ref,
-                 mixed_ref, grad_ref, small_sem, load_sem, table_sem, send_sem, recv_sem):
+                 mixed_ref, grad_ref, grad_size, small_sem, load_sem, table_sem, send_sem, recv_sem):
     place = Place(seq_count, ch_count)
     kernel_count, nuc_count = dilated_ref.shape[0], emb_ref.shape[0]
     width = cot_in.shape[1]
@@ -167,8 +177,12 @@
     par_send[pl.ds(nuc_count + kernel_count, kernel_count), :] = short_ref[...]
     tok_send[...] = tok_ref[...].astype(jnp.float32).astype(jnp.bfloat16)
     load_filt.wait()
+    largest = jnp.maximum(jnp.max(jnp.abs(filt_in[...]), axis=0, keepdims=True), LEAST)
+    filt_size[...] = largest
+    steps = steps_for(largest)
     for r in range(parts):
-        filt_send[pl.ds(r, width, stride=parts), :] = filt_in[pl.ds(r * LANES, LANES), :].T
+        turned[pl.ds(r, width, stride=parts), :] = (filt_in[pl.ds(r * LANES, LANES), :] * steps).T
+    filt_send[...] = fixed_point(turned[...].reshape(filt_send.shape))
     load_cot.wait()
     for r in range(parts):
         turned[pl.ds(r, width, stride=parts), :] = cot_in[pl.ds(r * LANES, LANES), :].astype(jnp.float32).T
@@ -191,27 +205,36 @@
     lax.fori_loop(1, seq_count, send_tokens, 0)
     pltpu.make_async_copy(tok_send, tok_all.at[place.s], recv_sem.at[1]).start()
 
-    def send(step, carry):
-        member, side, s = place.peer(step)
+    def send(side, step):
+        s = place.near(step)
+        member = side * seq_count + s
         chunk = place.chunk_of(member, place.side)
         device = place.device(side, s)
         pltpu.make_async_remote_copy(
-            src_ref=filt_send.at[rows_of(chunk)], dst_ref=filt_all.at[rows_of(place.g)], send_sem=send_sem.at[3],
+            src_ref=filt_send.at[chunk], dst_ref=filt_all.at[place.g], send_sem=send_sem.at[3],
             recv_sem=recv_sem.at[3], device_id=device, device_id_type=MESH).start()
         pltpu.make_async_remote_copy(
             src_ref=cot_send.at[chunk], dst_ref=cot_all.at[place.g], send_sem=send_sem.at[2],
             recv_sem=recv_sem.at[2], device_id=device, device_id_type=MESH).start()
+        pltpu.make_async_remote_copy(
+            src_ref=filt_size, dst_ref=filt_size_all.at[place.g], send_sem=send_sem.at[6],
+            recv_sem=recv_sem.at[6], device_id=device, device_id_type=MESH).start()
+
+    def send_four(index, carry):
+        step = seq_count // 2 - index
+        for far_step in (step, seq_count - step):
+            send(place.side, far_step)
+            send(1 - place.side, far_step)
         return carry
 
-    def send_pair(step, carry):
-        send(step, carry)
-        return send(members - step, carry)
-
-    lax.fori_loop(1, seq_count, send_pair, 0)
-    send(seq_count, 0)
+    send(place.side, seq_count // 2)
+    send(1 - place.side, seq_count // 2)
+    lax.fori_loop(1, seq_count // 2, send_four, 0)
+    send(1 - place.side, 0)
     own = place.chunk_of(place.g, place.side)
     pltpu.make_async_copy(cot_send.at[own], cot_all.at[place.g], recv_sem.at[2]).start()
-    pltpu.make_async_copy(filt_send.at[rows_of(own)], filt_all.at[rows_of(place.g)], recv_sem.at[3]).start()
+    pltpu.make_async_copy(filt_send.at[own], filt_all.at[place.g], recv_sem.at[3]).start()
+    pltpu.make_async_copy(filt_size, filt_size_all.at[place.g], recv_sem.at[6]).start()
 
     for table in tables:
         table.wait()
@@ -230,10 +253,11 @@
     tokens = jnp.concatenate([tokens, tokens], axis=1)
     turn_re, turn_im = twiddle_ref[0], twiddle_ref[1]
 
-    values = []
+    values, chosen = [], []
     for side in range(2):
         chunk = place.g if side == 0 else members - 1 - place.g
         here = par_lane == 2 * chunk + par_row // parts
+        chosen.append(here[None])
         values.append([
             jnp.sum(jnp.where(here, par_all[side, pl.ds(k, 1), :], 0.0), axis=1, keepdims=True)[None]
             for k in range(nuc_count + 2 * kernel_count)
@@ -278,11 +302,13 @@
         transform([fir(side, side, 1), fir(side, 1 - side, -1)], (8 * side, 8 * side + 2))
     await_bytes(cot_all, recv_sem.at[2])
     await_bytes(filt_all, recv_sem.at[3])
+    await_bytes(filt_size_all, recv_sem.at[6])
     for side in range(2):
         block = slice(side * seq_count, (side + 1) * seq_count)
         seed = cot_all[block].astype(jnp.float32) * hidden_ref[side]
-        filt = filt_all[side * seq_count * TILE:(side + 1) * seq_count * TILE]
-        transform([filt, seed.reshape(flat)], (8 * side + 4, 8 * side + 6))
+        size = jnp.sum(jnp.where(chosen[side], filt_size_all[block], 0.0), axis=2, keepdims=True)
+        filt = floating(filt_all[block]) * (size * (1.0 / COUNTS))
+        transform([filt.reshape(flat), seed.reshape(flat)], (8 * side + 4, 8 * side + 6))
 
     def parts_of(side, kind, jj):
         full = spec_ref[8 * side + 2 * kind + jj]
@@ -317,7 +343,13 @@
         wave = dot_left(first_back_ref, jnp.concatenate(columns, axis=1))
         block = slice(side * seq_count, (side + 1) * seq_count)
         mixed_ref[block] = (hidden_ref[side] * wave[:, :LANES].reshape(tiles)).astype(jnp.bfloat16)
-        grad_ref[side * seq_count * TILE:(side + 1) * seq_count * TILE] = wave[:, LANES:]
+        grad = wave[:, LANES:].reshape(tiles)
+        largest = [
+            jnp.maximum(jnp.max(jnp.where(row // parts == jj, jnp.abs(grad), 0.0), axis=(1, 2), keepdims=True), LEAST)
+            for jj in range(2)
+        ]
+        grad_size[block] = jnp.where(lane[:, :1] < LANES // 2, largest[0], largest[1])
+        grad_ref[block] = fixed_point(grad * jnp.where(row < parts, steps_for(largest[0]), steps_for(largest[1])))
 
         def give_back(step, carry):
             s = place.near(step)
@@ -325,24 +357,29 @@
             member = side * seq_count + s
             chunk = place.chunk_of(place.g, side)
             pltpu.make_async_remote_copy(
-                src_ref=grad_ref.at[rows_of(member)], dst_ref=grad_all.at[rows_of(chunk)], send_sem=send_sem.at[5],
+                src_ref=grad_ref.at[member], dst_ref=grad_all.at[chunk], send_sem=send_sem.at[5],
                 recv_sem=recv_sem.at[5], device_id=device, device_id_type=MESH).start()
             pltpu.make_async_remote_copy(
                 src_ref=mixed_ref.at[member], dst_ref=mixed_all.at[chunk], send_sem=send_sem.at[4],
                 recv_sem=recv_sem.at[4], device_id=device, device_id_type=MESH).start()
+            pltpu.make_async_remote_copy(
+                src_ref=grad_size.at[member], dst_ref=grad_size_all.at[chunk], send_sem=send_sem.at[7],
+                recv_sem=recv_sem.at[7], device_id=device, device_id_type=MESH).start()
             return carry
 
-        def give_pair(step, carry):
+        def give_pair(index, carry):
+            step = seq_count // 2 - index
             give_back(step, carry)
             return give_back(seq_count - step, carry)
 
+        give_back(seq_count // 2, 0)
         lax.fori_loop(1, seq_count // 2, give_pair, 0)
-        give_back(seq_count // 2, 0)
 
         @pl.when(place.side == side)
         def _():
             pltpu.make_async_copy(mixed_ref.at[place.g], mixed_all.at[own], recv_sem.at[4]).start()
-            pltpu.make_async_copy(grad_ref.at[rows_of(place.g)], grad_all.at[rows_of(own)], recv_sem.at[5]).start()
+            pltpu.make_async_copy(grad_ref.at[place.g], grad_all.at[own], recv_sem.at[5]).start()
+            pltpu.make_async_copy(grad_size.at[place.g], grad_size_all.at[own], recv_sem.at[7]).start()
 
         @pl.when(place.side != side)
         def _():
@@ -350,27 +387,45 @@
 
     await_bytes(tok_all.at[pl.ds(0, seq_count - 1)], send_sem.at[1])
     await_bytes(cot_send.at[pl.ds(0, members - 1)], send_sem.at[2])
-    await_bytes(filt_send.at[pl.ds(0, TILE * (members - 1))], send_sem.at[3])
+    await_bytes(filt_send.at[pl.ds(0, members - 1)], send_sem.at[3])
+    await_bytes(filt_size_all.at[pl.ds(0, members - 1)], send_sem.at[6])
     await_bytes(mixed_ref.at[pl.ds(0, members - 1)], send_sem.at[4])
-    await_bytes(grad_ref.at[pl.ds(0, TILE * (members - 1))], send_sem.at[5])
+    await_bytes(grad_ref.at[pl.ds(0, members - 1)], send_sem.at[5])
+    await_bytes(grad_size.at[pl.ds(0, members - 1)], send_sem.at[7])
     await_bytes(mixed_all, recv_sem.at[4])
     await_bytes(grad_all, recv_sem.at[5])
-
-
-def settle_kernel(mixed_hbm, grad_hbm, mixed_ref, grad_ref, mixed_all, grad_all, turned, sem):
+    await_bytes(grad_size_all, recv_sem.at[7])
+
+
+def settle_kernel(mixed_hbm, grad_hbm, size_hbm, mixed_out, grad_out, mixed_all, grad_all, size_all, turned, mixed_ref, grad_ref,
+                  load_sem, store_sem):
     parts = grad_ref.shape[0] // LANES
     width = grad_ref.shape[1]
-    load_mixed = pltpu.make_async_copy(mixed_hbm, mixed_all, sem.at[0])
-    load_grad = pltpu.make_async_copy(grad_hbm, grad_all, sem.at[1])
-    load_mixed.start()
-    load_grad.start()
-    load_mixed.wait()
-    turned[...] = mixed_all[...].astype(jnp.float32).reshape(turned.shape)
-    for r in range(parts):
-        mixed_ref[pl.ds(r * LANES, LANES), :] = turned[pl.ds(r, width, stride=parts), :].T.astype(jnp.bfloat16)
-    load_grad.wait()
-    for r in range(parts):
-        grad_ref[pl.ds(r * LANES, LANES), :] = grad_all[pl.ds(r, width, stride=parts), :].T
+    loads = [
+        pltpu.make_async_copy(far, near, load_sem.at[index])
+        for index, (far, near) in enumerate([(mixed_hbm, mixed_all), (grad_hbm, grad_all), (size_hbm, size_all)])
+    ]
+    for load in loads:
+        load.start()
+    row = lax.broadcasted_iota(jnp.int32, (1, TILE, LANES), 1)
+    stores = []
+
+    def turn(values, into, out, sem):
+        turned[...] = values.reshape(turned.shape)
+        for r in range(parts):
+            into[pl.ds(r * LANES, LANES), :] = turned[pl.ds(r, width, stride=parts), :].T.astype(into.dtype)
+        stores.append(pltpu.make_async_copy(into, out, sem))
+        stores[-1].start()
+
+    loads[0].wait()
+    turn(mixed_all[...].astype(jnp.float32), mixed_ref, mixed_out, store_sem.at[0])
+    loads[1].wait()
+    loads[2].wait()
+    size = size_all[...] * (1.0 / COUNTS)
+    size = jnp.where(row < parts, size[:, :, :1], size[:, :, LANES - 1:])
+    turn(floating(grad_all[...]) * size, grad_ref, grad_out, store_sem.at[1])
+    for store in stores:
+        store.wait()
 
 
 def local(seq_count, ch_count, tokens, embedding, taps_dilated, taps_short, long_filter, cotangent):
@@ -382,17 +437,21 @@
     rows = parts * seq_count
     assert 2 * parts == TILE and width == 2 * members
     vmem = pl.BlockSpec(memory_space=pltpu.VMEM)
-    f32, bf16 = jnp.float32, jnp.bfloat16
+    f32, bf16, i16 = jnp.float32, jnp.bfloat16, jnp.int16
     shape = jax.ShapeDtypeStruct
     limit = 67043328
 
     far = pl.BlockSpec(memory_space=pltpu.HBM)
     tables = [jnp.asarray(t) for t in dft_tables(seq_count, parts)]
-    mixed_all, grad_all = pl.pallas_call(
+    returned = pl.pallas_call(
         functools.partial(whole_kernel, seq_count, ch_count),
-        out_shape=(shape((members, TILE, LANES), bf16), shape((members * TILE, LANES), f32)),
+        out_shape=(
+            shape((members, TILE, LANES), bf16),
+            shape((members, TILE, LANES), i16),
+            shape((members, 1, LANES), f32),
+        ),
         in_specs=[far] * 11,
-        out_specs=(far,) * 2,
+        out_specs=(far,) * 3,
         scratch_shapes=[
             pltpu.VMEM((parts, LANES), jnp.int32),
             pltpu.VMEM(embedding.shape, bf16),
@@ -404,21 +463,24 @@
             pltpu.VMEM((parts, LANES), bf16),
             pltpu.VMEM((-(-(nuc_count + 2 * kernel_count) // TILE) * TILE, width), f32),
             pltpu.VMEM((members, TILE, LANES), bf16),
-            pltpu.VMEM((members * TILE, LANES), f32),
+            pltpu.VMEM((members, TILE, LANES), i16),
+            pltpu.VMEM((1, width), f32),
             pltpu.VMEM((seq_count, parts, LANES), bf16),
             pltpu.VMEM((2, -(-(nuc_count + 2 * kernel_count) // TILE) * TILE, width), f32),
             pltpu.VMEM((members, TILE, LANES), bf16),
-            pltpu.VMEM((members * TILE, LANES), f32),
+            pltpu.VMEM((members, TILE, LANES), i16),
+            pltpu.VMEM((members, 1, width), f32),
             *[pltpu.VMEM(t.shape, t.dtype) for t in tables],
             pltpu.VMEM((2, seq_count, TILE, LANES), f32),
             pltpu.VMEM((16, rows, 2 * LANES), f32),
             pltpu.VMEM((members, TILE, LANES), bf16),
-            pltpu.VMEM((members * TILE, LANES), f32),
+            pltpu.VMEM((members, TILE, LANES), i16),
+            pltpu.VMEM((members, 1, LANES), f32),
             pltpu.SemaphoreType.DMA((4,)),
             pltpu.SemaphoreType.DMA((3,)),
             pltpu.SemaphoreType.DMA((5,)),
-            pltpu.SemaphoreType.DMA((6,)),
-            pltpu.SemaphoreType.DMA((6,)),
+            pltpu.SemaphoreType.DMA((8,)),
+            pltpu.SemaphoreType.DMA((8,)),
         ],
         compiler_params=pltpu.CompilerParams(collective_id=0, has_side_effects=True, vmem_limit_bytes=limit),
         name="whole",
@@ -427,17 +489,21 @@
     return pl.pallas_call(
         settle_kernel,
         out_shape=(shape((block_rows, width), bf16), shape((block_rows, width), f32)),
-        in_specs=[far] * 2,
-        out_specs=(vmem,) * 2,
+        in_specs=[far] * 3,
+        out_specs=(far,) * 2,
         scratch_shapes=[
             pltpu.VMEM((members, TILE, LANES), bf16),
+            pltpu.VMEM((members, TILE, LANES), i16),
+            pltpu.VMEM((members, 1, LANES), f32),
             pltpu.VMEM((members * TILE, LANES), f32),
-            pltpu.VMEM((members * TILE, LANES), f32),
+            pltpu.VMEM((block_rows, width), bf16),
+            pltpu.VMEM((block_rows, width), f32),
+            pltpu.SemaphoreType.DMA((3,)),
             pltpu.SemaphoreType.DMA((2,)),
         ],
         compiler_params=pltpu.CompilerParams(vmem_limit_bytes=limit),
         name="settle",
-    )(mixed_all, grad_all)
+    )(*returned)
 
 
 def solution(mesh):

time: 43.5 us -> 39.4 us (0.906); the launches traced: 42.7 us -> 39.3 us
  Pallas kernels: 42.1 us -> 38.7 us
    pallas_call x1, Pallas kernels: 40.2 us -> 36.6 us  [local(): pl.pallas_call(functools.partial(whole_kernel, seq_count, ch_count), out_...]
where the time goes in v3:
time: 39.4 us; the launch traced here: 39.3 us
  Pallas kernels  38.7 us (98%)
  between operations  0.64 us (2%)
    pallas_call x1, Pallas kernels, local(): pl.pallas_call(functools.partial(whole_kernel, seq_count, ch_count), out_...  36.6 us
    pallas_call x1, Pallas kernels, local(): pl.pallas_call(settle_kernel, out_shape=(shape((block_rows, width), bf16)...  2.1 us

profile of v3, /device:TPU:1, one launch (start us, length us, event | category | flops | bytes accessed | tf_op | source)
XLA Modules:
  0.0 39.3 jit_solution(11031467760764730024)
XLA Ops:
  0.6 36.6 %whole.1 = (bf16[64,8,128]{2,1,0:T(8,128)(2,1)}, s16[64,8,128]{2,1,0:T(8,128)(2,1)}, f32[64,1,128]{2,1,0:T(1,128)}) custom-call(s32[4,128]{1,0:T(4,128)} %bitcast.1, bf16[5,128]{1,0:T(8,128)(2,1)} %emb_hbm.1, f32[3,128]{1,0:T(4,128)} %dilated_hbm.1, f32[3,128]{1,0:T(4,128)} %short_hbm.1, bf16[512,128]{1,0:T(8,128)(2,1)} %cot_hbm.1, f32[512,128]{1,0:T(8,128)} %filt_hbm.1, ...), custom_call_target="tpu_custom_call" | custom-call | tf_op jit(solution)/shard_map/whole/pallas_call | solution.py:446
  37.2 2.1 %settle.1 = (bf16[512,128]{1,0:T(8,128)(2,1)}, f32[512,128]{1,0:T(8,128)}) custom-call(bf16[64,8,128]{2,1,0:T(8,128)(2,1)} %get-tuple-element.5.mixed_hbm, s16[64,8,128]{2,1,0:T(8,128)(2,1)} %get-tuple-element.6.grad_hbm, f32[64,1,128]{2,1,0:T(1,128)} %get-tuple-element.7.size_hbm), custom_call_target="tpu_custom_call" | custom-call | tf_op jit(solution)/shard_map/settle/pallas_call | solution.py:489
